TPU v7x, 256 devices: a whole 4x4x8 slice. The times are simulated.
256 devices in a mesh: rows: 32 (over y, x, core), cols: 8 (over z).
Axes of the slice: x: 4, y: 4, z: 8, core: 2. Of those that a mesh axis runs over, the one named last changes fastest.
Arguments:
- weight: bfloat16 [49152, 12288], P('rows', 'cols'), may hold values from -6 to 6
- inverse_panel: float32 [256, 12288], P('rows', 'cols'), as said below
- keep_blocks: int32 [768, 4], P('rows'), may hold values 0 or 1
- calibration: bfloat16 [1536, 12288], P('rows', 'cols'), may hold values from -0.0546875 to 0.0546875
Outputs:
- pruned: bfloat16 [49152, 12288], P('rows', 'cols')
- next_input: bfloat16 [1536, 49152], P('cols', 'rows')
Inputs may be any that keep to these rules, and one draw needn't show every extreme that they name: inverse_panel is upper triangular: entry (j, k) is zero for k < j; its diagonal lies between 1 and 3.
All inputs are finite; a program needn't handle non-finite values. No bound on the sum of `keep_blocks` on one device may be relied on, other than what follows from the above.
Results may differ from a plain program's by a relative error of at most 0.017.
Values may be sent and summed in bfloat16 or wider, within the bound.
A program may use at most 64 MiB of HBM per device.

v0:
```python
import jax
import jax.numpy as jnp
from jax import lax
from jax.experimental import pallas as pl
from jax.experimental.pallas import tpu as pltpu
from jax.sharding import PartitionSpec as P

TILE = 64
WIN = 256
F32 = jnp.float32
BF16 = jnp.bfloat16


def dot_exact(a, b):
    return lax.dot_general(
        a, b, (((1,), (0,)), ((), ())), precision=lax.Precision.HIGHEST, preferred_element_type=F32
    )


def invert_blocks(square):
    row = lax.broadcasted_iota(jnp.int32, (WIN, WIN), 0)
    col = lax.broadcasted_iota(jnp.int32, (WIN, WIN), 1)
    inverse = jnp.where(row == col, 1.0 / jnp.where(row == col, square, 1.0), 0.0)
    size = 1
    while size < TILE:
        corner = ((row // size) % 2 == 0) & (col // size == row // size + 1)
        inverse = inverse - dot_exact(dot_exact(inverse, jnp.where(corner, square, 0.0)), inverse)
        size *= 2
    return inverse


def solve_rows(weight, kept, inverse, coupling):
    col_tile = lax.broadcasted_iota(jnp.int32, weight.shape, 1) // TILE
    whole = dot_exact(weight, inverse)
    errors = jnp.where((col_tile == 0) & ~kept, whole, 0.0)
    for tile in range(1, WIN // TILE):
        now = whole - dot_exact(errors, coupling)
        errors = jnp.where((col_tile == tile) & ~kept, now, errors)
    return errors


def coupling_of(square, inverse):
    row = lax.broadcasted_iota(jnp.int32, (WIN, WIN), 0) // TILE
    col = lax.broadcasted_iota(jnp.int32, (WIN, WIN), 1) // TILE
    return dot_exact(jnp.where(row < col, square, 0.0), inverse)


def solve_kernel(weight_ref, square_ref, keep_ref, errors_ref):
    inverse = invert_blocks(square_ref[...])
    coupling = coupling_of(square_ref[...], inverse)
    groups = keep_ref.shape[0]
    lane_tile = lax.broadcasted_iota(jnp.int32, (groups, WIN), 1) // TILE
    kept = jnp.zeros((groups, WIN), jnp.int32)
    for tile in range(WIN // TILE):
        kept = jnp.where(lane_tile == tile, keep_ref[:, tile : tile + 1], kept)
    step = 6
    for first in range(0, groups, step):
        rows = pl.ds(first * TILE, step * TILE)
        mask = jnp.concatenate(
            [jnp.broadcast_to(kept[g : g + 1], (TILE, WIN)) for g in range(first, first + step)], axis=0
        )
        errors = solve_rows(weight_ref[rows, :].astype(F32), mask != 0, inverse, coupling)
        errors_ref[rows, :] = errors.astype(BF16)


def per_device(weight, inverse_panel, keep_blocks, calibration):
    gathered = lax.all_gather(inverse_panel.astype(BF16), "rows", axis=0, tiled=True)
    owner = lax.axis_index("cols") == 0
    square = jnp.where(owner, gathered[:, :WIN].astype(F32), jnp.eye(WIN, dtype=F32))
    local_errors = pl.pallas_call(
        solve_kernel,
        grid=(1,),
        out_shape=jax.ShapeDtypeStruct((weight.shape[0], WIN), BF16),
        in_specs=[
            pl.BlockSpec((weight.shape[0], WIN), lambda i: (0, 0)),
            pl.BlockSpec((WIN, WIN), lambda i: (0, 0)),
            pl.BlockSpec(keep_blocks.shape, lambda i: (0, 0)),
        ],
        out_specs=pl.BlockSpec((weight.shape[0], WIN), lambda i: (0, 0)),
        compiler_params=pltpu.CompilerParams(vmem_limit_bytes=40 << 20),
    )(weight, square, keep_blocks)
    errors = lax.psum(jnp.where(owner, local_errors, jnp.zeros_like(local_errors)), "cols")
    update = lax.dot_general(errors, gathered, (((1,), (0,)), ((), ())), preferred_element_type=F32)
    updated = weight.astype(F32) - update
    keep_full = jnp.repeat(jnp.repeat(keep_blocks.astype(F32), TILE, axis=0), TILE, axis=1)
    keep_padded = jnp.pad(keep_full, ((0, 0), (0, weight.shape[1] - WIN)), constant_values=1.0)
    window_scale = jnp.where(owner, keep_padded, F32(1.0))
    pruned = (updated * window_scale).astype(BF16)
    partial_terms = lax.dot_general(
        lax.all_gather(calibration, "rows", axis=0, tiled=True),
        pruned,
        (((1,), (1,)), ((), ())),
        preferred_element_type=F32,
    )
    next_input = lax.psum_scatter(partial_terms.astype(BF16), "cols", scatter_dimension=0, tiled=True)
    return (pruned, next_input)


def solution(mesh):
    in_specs = (P("rows", "cols"), P("rows", "cols"), P("rows", None), P("rows", "cols"))
    out_specs = (P("rows", "cols"), P("cols", "rows"))
    return jax.shard_map(
        per_device, mesh=mesh, in_specs=in_specs, out_specs=out_specs, check_vma=False
    )
```

profile of v0, /device:TPU:8, one launch (start us, length us, event | category | flops | bytes accessed | tf_op | source)
XLA Modules:
  0.0 219.8 jit_solution(6410754318576128293)
XLA Ops:
  8.0 0.0 all-reduce.3.cloned.1.call-start
  8.0 0.8 copy.12.keep_ref
  8.8 0.8 convert_element_type.25
  9.6 24.9 %all_gather.6 = bf16[256,1536]{1,0:T(8,128)(2,1)S(1)} all-gather(bf16[8,1536]{1,0:T(8,128)(2,1)S(1)} %convert_element_type.25), channel_id=1, replica_groups=mesh['rows'=32,'cols'=8] {'rows'}, dimensions={0}, use_global_device_ids=true | all-gather | bytes 811008 | tf_op jit(solution)/shard_map/all_gather | solution.py:67
  34.6 0.0 copy-start
  34.6 2.6 %copy-done = bf16[1536,1536]{1,0:T(8,128)(2,1)S(1)} copy-done((bf16[1536,1536]{1,0:T(8,128)(2,1)S(1)}, bf16[1536,1536]{1,0:T(8,128)(2,1)}, u32[]{:S(2)}) %copy-start) | copy-done | bytes 4718616
  37.2 14.0 %shard_map.59 = bf16[1536,256]{1,0:T(8,128)(2,1)S(1)} custom-call(bf16[1536,1536]{1,0:T(8,128)(2,1)S(1)} %copy-done, f32[256,256]{1,0:T(8,128)S(1)} %convert_select_fusion.square_ref, s32[24,4]{1,0:T(8,128)S(1)} %copy.12.keep_ref), custom_call_target="tpu_custom_call" | custom-call | tf_op jit(solution)/shard_map/pallas_call | solution.py:70
  51.2 0.9 broadcast_select_fusion
  52.1 0.0 all-reduce.3.cloned.1.call-update
  52.2 0.0 all-gather.2.cloned.1.call-start
  52.2 0.5 all-gather.2.cloned.1.call-update
  52.7 0.0 reduce-scatter.4.cloned.1.call-start
  52.8 0.0 copy-done.2
  52.8 0.1 broadcast_in_dim.14
  52.9 0.0 copy-done.1
  52.9 0.1 reshape.10
  53.0 0.2 broadcast_in_dim.15
  53.2 0.5 copy.13
  53.6 74.6 %all-reduce.3.cloned.1.call-done = bf16[1536,256]{1,0:T(8,128)(2,1)} async-done(((bf16[1536,256]{1,0:T(8,128)(2,1)}), bf16[1536,256]{1,0:T(8,128)(2,1)}) %all-reduce.3.cloned.1.call-update) | async-done | bytes 786448 | tf_op jit(solution)/shard_map/psum | solution.py:82
  128.2 6.4 %fusion.1 = bf16[1536,1536]{1,0:T(8,128)(2,1)} fusion(f32[1536,256]{1,0:T(8,128)S(1)} %copy.13, bf16[1536,256]{1,0:T(8,128)(2,1)} %all-reduce.3.cloned.1.call-done, bf16[256,1536]{1,0:T(8,128)(2,1)} %copy-done.1, bf16[1536,1536]{1,0:T(8,128)(2,1)} %weight_ref.1, pred[]{:T(512)S(6)} %eq.6), kind=kOutput, calls=%fused_computation.2 | convolution fusion | flops 1219756032 | bytes 12582913 | tf_op jit(solution)/shard_map/dot_general | solution.py:83
  134.6 12.3 %fusion.2 = bf16[1536,1536]{0,1:T(8,128)(2,1)} fusion(bf16[1536,1536]{1,0:T(8,128)(2,1)} %fusion.1, bf16[1536,1536]{1,0:T(8,128)(2,1)} %all-gather.2.cloned.1.call-done), kind=kOutput, calls=%fused_computation.4 | convolution fusion | flops 7250116608 | bytes 14155776 | tf_op jit(solution)/shard_map/dot_general | solution.py:89
  146.9 6.6 %copy.15 = bf16[1536,1536]{1,0:T(8,128)(2,1)} copy(bf16[1536,1536]{0,1:T(8,128)(2,1)} %fusion.2) | data formatting | bytes 9437184
  153.6 0.0 reduce-scatter.4.cloned.1.call-update
  153.6 58.8 %reduce-scatter.4.cloned.1.call-done = bf16[192,1536]{1,0:T(8,128)(2,1)} async-done(((bf16[1536,1536]{1,0:T(8,128)(2,1)}), bf16[192,1536]{1,0:T(8,128)(2,1)}) %reduce-scatter.4.cloned.1.call-update) | async-done | bytes 589840
  (5 shorter events, 0.0 us)
Async XLA Ops:
  8.0 120.2 %all-reduce.3.cloned.1.call-start = ((), (), s32[]{:S(2)}) async-start(), calls=%async_computation.1 | async-start | bytes 1572864 | tf_op jit(solution)/shard_map/psum | solution.py:82
  9.6 43.2 %copy-start.2 = (s32[24,4]{0,1:T(4,128)S(1)}, s32[24,4]{0,1:T(4,128)}, u32[]{:S(2)}) copy-start(s32[24,4]{0,1:T(4,128)} %param.6) | copy-start | bytes 1156
  34.5 18.4 %copy-start.1 = (bf16[256,1536]{1,0:T(8,128)(2,1)}, bf16[256,1536]{1,0:T(8,128)(2,1)S(1)}, u32[]{:S(2)}) copy-start(bf16[256,1536]{1,0:T(8,128)(2,1)S(1)} %all_gather.6) | copy-start | bytes 2359300
  34.6 2.6 %copy-start = (bf16[1536,1536]{1,0:T(8,128)(2,1)S(1)}, bf16[1536,1536]{1,0:T(8,128)(2,1)}, u32[]{:S(2)}) copy-start(bf16[1536,1536]{1,0:T(8,128)(2,1)} %weight_ref.1) | copy-start | bytes 14155780
  52.2 82.5 %all-gather.2.cloned.1.call-start = ((), (), s32[]{:S(2)}) async-start(), calls=%async_computation.2 | async-start | bytes 4866048 | tf_op jit(solution)/shard_map/all_gather | solution.py:90
  52.7 159.6 %reduce-scatter.4.cloned.1.call-start = ((), (), s32[]{:S(2)}) async-start(), calls=%async_computation.3 | async-start | bytes 5308416
Sparse Core Ops, SparseCore 0:
  52.3 75.8 all-reduce.2
  153.7 58.6 reduce-scatter.3
Sparse Core Ops, SparseCore 1:
  55.5 52.8 all-gather.1
where the time goes:
time: 221 us; the launch traced here: 220 us
  waiting for transfers between devices  134 us (61%)
  blocking collectives  24.9 us (11%)
  matrix products  18.7 us (8%)
  between operations  15.5 us (7%)
  Pallas kernels  14 us (6%)
  local copies, waits for them, and re-layouts  10.8 us (5%)
    psum x1, waiting for transfers between devices, per_device(): lax.psum(jnp.where(owner, local_errors, jnp.zeros_like(local_errors)), 'c...  74.6 us
    unnamed x4, waiting for transfers between devices  59.3 us
    all_gather x1, blocking collectives, per_device(): lax.all_gather(inverse_panel.astype(BF16), 'rows', axis=0, tiled=True)  24.9 us
    pallas_call x1, Pallas kernels, per_device(): pl.pallas_call(solve_kernel, grid=(1,), out_shape=jax.ShapeDtypeStruct((w...  14 us
    dot_general x1, matrix products, per_device(): lax.dot_general(lax.all_gather(calibration, 'rows', axis=0, tiled=True),...  12.3 us
    unnamed x8, local copies, waits for them, and re-layouts  10 us
    dot_general x1, matrix products, per_device(): lax.dot_general(errors, gathered, (((1,), (0,)), ((), ())), preferred_ele...  6.41 us
  transfers between devices with their start and end apart: 3, of which 2 were waited for; matrix products, arithmetic and copies ran while one was open for 3% of the time, Pallas kernels for 0%

commit v1 on v0

v1 whole, which is shorter than its diff:
```python
import functools

import jax
import jax.numpy as jnp
from jax import lax
from jax.experimental import pallas as pl
from jax.experimental.pallas import tpu as pltpu
from jax.sharding import PartitionSpec as P

TILE = 64
WIN = 256
F32 = jnp.float32
BF16 = jnp.bfloat16
MESH = pl.DeviceIdType.MESH

SIDE = 4
PLANE = 32
DEPTH = 8
TOKENS = 48
HALF = 768
BLOCK_TOKENS = 192
SUB = 256
SUBS = 3
LINK = 64
LINKS = HALF // LINK
HOP = 3
TICK0, TICK = 1.0, 0.65
ON = "gswcptr"


def dot_exact(a, b):
    return lax.dot_general(
        a, b, (((1,), (0,)), ((), ())), precision=lax.Precision.HIGHEST, preferred_element_type=F32
    )


def coupling_of(square, inverse):
    row = lax.broadcasted_iota(jnp.int32, (WIN, WIN), 0) // TILE
    col = lax.broadcasted_iota(jnp.int32, (WIN, WIN), 1) // TILE
    return dot_exact(jnp.where(row < col, square, 0.0), inverse)


def solve_rows(weight, kept, inverse, coupling):
    col_tile = lax.broadcasted_iota(jnp.int32, weight.shape, 1) // TILE
    whole = dot_exact(weight, inverse)
    errors = jnp.where((col_tile == 0) & ~kept, whole, 0.0)
    for tile in range(1, WIN // TILE):
        now = whole - dot_exact(errors, coupling)
        errors = jnp.where((col_tile == tile) & ~kept, now, errors)
    return errors


def fused_kernel(
    weight, panel, keep, calib, pruned, next_input,
    gath, w_v, window, panel_v, sq, inv_v, cpl_v, factor, kept_v, scale_v, errors_v, terms, ring,
    gsend, grecv, ssend, srecv, zsend, zrecv, wsend, wrecv, rsend, rrecv, local, psem,
):
    r, z = lax.axis_index("rows"), lax.axis_index("cols")
    core, x, y = lax.rem(r, 2), lax.rem(lax.div(r, 2), SIDE), lax.div(r, 2 * SIDE)
    near = lax.div(z, DEPTH // 2)

    def moved(a, b):
        down, right = a * core + b * (1 - core), a * (1 - core) + b * core
        return (lax.rem(y + down, SIDE) * SIDE + lax.rem(x + right, SIDE)) * 2 + core

    def onward(way):
        return lax.rem(z + 1 + way * (DEPTH - 2), DEPTH)

    other = r + 1 - 2 * core

    calib_left = pltpu.make_async_copy(calib.at[:, pl.ds(0, HALF)], gath.at[r, pl.ds(0, TOKENS)], local.at[0])
    calib_right = pltpu.make_async_copy(
        calib.at[:, pl.ds(HALF, HALF)], gath.at[r, pl.ds(TOKENS, TOKENS)], local.at[1]
    )
    panel_load = pltpu.make_async_copy(panel, panel_v, local.at[2])
    weight_load = pltpu.make_async_copy(weight, w_v, local.at[3])
    window_load = pltpu.make_async_copy(weight.at[:, pl.ds(0, WIN)], window, local.at[4])
    panel_load.start()
    calib_left.start()
    calib_right.start()

    @pl.when(z == 0)
    def _():
        window_load.start()

    weight_load.start()

    barrier = pltpu.get_barrier_semaphore()

    def greet_plane(k, carry):
        pl.semaphore_signal(barrier, inc=1, device_id=(lax.rem(r + k, PLANE), z), device_id_type=MESH)
        return carry

    def greet_column(k, carry):
        pl.semaphore_signal(barrier, inc=1, device_id=(r, lax.rem(z + k, DEPTH)), device_id_type=MESH)
        return carry

    lax.fori_loop(1, PLANE, greet_plane, 0)
    lax.fori_loop(1, DEPTH, greet_column, 0)
    panel_load.wait()

    rows8 = panel_v[...]
    gath[r, pl.ds(2 * TOKENS, 16), :] = jnp.concatenate([rows8[:, :HALF], rows8[:, HALF:]], axis=0).astype(BF16)

    @pl.when(z == 0)
    def _():
        sq[r] = panel_v[:, pl.ds(0, WIN)]

    groups = keep.shape[0]
    lane_tile = lax.broadcasted_iota(jnp.int32, (groups, WIN), 1) // TILE
    kept = jnp.zeros((groups, WIN), jnp.int32)
    for tile in range(WIN // TILE):
        kept = jnp.where(lane_tile == tile, keep[:, tile : tile + 1], kept)
    kept_v[...] = kept
    scale_v[...] = jnp.where(z == 0, kept, 1)

    calib_left.wait()
    calib_right.wait()
    pl.semaphore_wait(barrier, PLANE - 1 + DEPTH - 1)

    def square_down(k):
        return pltpu.make_async_remote_copy(
            src_ref=sq.at[r], dst_ref=sq.at[r], send_sem=zsend.at[k - 1], recv_sem=zrecv.at[0],
            device_id=(r, lax.rem(z + k, DEPTH)), device_id_type=MESH,
        )

    def square_across(k, slot):
        return pltpu.make_async_remote_copy(
            src_ref=sq.at[slot], dst_ref=sq.at[slot], send_sem=ssend.at[k - 1], recv_sem=srecv.at[slot],
            device_id=(lax.rem(r + k, PLANE), z), device_id_type=MESH,
        )

    def shard(slot, sem, to):
        return pltpu.make_async_remote_copy(
            src_ref=gath.at[slot], dst_ref=gath.at[slot], send_sem=gsend.at[sem], recv_sem=grecv.at[slot],
            device_id=(to, z), device_id_type=MESH,
        )

    def link(way, i):
        rows = pl.ds(pl.multiple_of(way * HALF + i * LINK, LINK), LINK)
        return pltpu.make_async_remote_copy(
            src_ref=window.at[rows], dst_ref=window.at[rows], send_sem=wsend.at[way, i], recv_sem=wrecv.at[way, i],
            device_id=(r, onward(way)), device_id_type=MESH,
        )

    def piece(way, sub, step):
        return pltpu.make_async_remote_copy(
            src_ref=ring.at[way, sub, step], dst_ref=ring.at[way, sub, step + 1],
            send_sem=rsend.at[way, sub, step], recv_sem=rrecv.at[way, sub, step],
            device_id=(r, onward(way)), device_id_type=MESH,
        )

    def block_of(way, step):
        ahead = lax.rem(z + DEPTH - 1 - step + way * (2 * step + 2 - DEPTH), DEPTH)
        return pl.multiple_of(ahead * BLOCK_TOKENS, BLOCK_TOKENS)

    handed = []

    def give(slot, to):
        handed.append(None)
        shard(slot, len(handed) - 1, to).start()

    def first_sends():
        @pl.when(z == 0)
        def _():
            for k in range(1, DEPTH):
                square_down(k).start()
            window_load.wait()

            def send(i, carry):
                link(0, i).start()
                link(1, i).start()
                return carry

            lax.fori_loop(0, LINKS, send, 0)

        for k in (1, 3):
            give(r, moved(k, 0))
            give(r, moved(0, k))
        give(r, moved(2, 0))
        give(r, other)

    def squares_on():
        @pl.when(z != 0)
        def _():
            square_down(1).wait_recv()

        def send(k, carry):
            square_across(k, r).start()
            return carry

        lax.fori_loop(1, PLANE, send, 0)

    def take_squares():
        def take(k, carry):
            square_across(k, lax.rem(r + PLANE - k, PLANE)).wait_recv()
            return carry

        lax.fori_loop(1, PLANE, take, 0)

    def along_first(j):
        slot = moved(SIDE - j, 0)
        shard(slot, 0, other).wait_recv()
        for k in (1, 3):
            give(slot, moved(0, k))
        give(slot, other)

    def along_second(j, k):
        slot = moved(SIDE - j, SIDE - k)
        shard(slot, 0, other).wait_recv()
        if (k == 1 and j in (0, 1)) or (k == 3 and j in (2, 3)):
            give(slot, moved(0, k))
        give(slot, other)

    def take_other():
        def take(q, carry):
            shard(2 * q + 1 - core, 0, other).wait_recv()
            return carry

        lax.fori_loop(0, PLANE // 2, take, 0)

    def tick(n):
        for way in range(2):
            hops = z if way == 0 else DEPTH - z
            i = n - HOP * hops

            @pl.when((z != 0) & (i >= 0) & (i < LINKS))
            def _(way=way, i=i, hops=hops):
                link(way, i).wait_recv()

                @pl.when(hops != DEPTH - 1)
                def _():
                    link(way, i).start()

    def invert_start():
        row = lax.broadcasted_iota(jnp.int32, (WIN, WIN), 0)
        col = lax.broadcasted_iota(jnp.int32, (WIN, WIN), 1)
        square = sq[...].reshape(WIN, WIN)
        inv_v[...] = jnp.where(row == col, 1.0 / jnp.where(row == col, square, 1.0), 0.0)

    def invert_level(size):
        row = lax.broadcasted_iota(jnp.int32, (WIN, WIN), 0)
        col = lax.broadcasted_iota(jnp.int32, (WIN, WIN), 1)
        square = sq[...].reshape(WIN, WIN)
        inverse = inv_v[...]
        corner = ((row // size) % 2 == 0) & (col // size == row // size + 1)
        inv_v[...] = inverse - dot_exact(dot_exact(inverse, jnp.where(corner, square, 0.0)), inverse)

    def couple():
        cpl_v[...] = coupling_of(sq[...].reshape(WIN, WIN), inv_v[...])

    def expand(ref, first):
        group = lax.div(first, TILE)
        return jnp.concatenate(
            [jnp.broadcast_to(ref[pl.ds(group + g, 1), :], (TILE, WIN)) for g in range(SUB // TILE)], axis=0
        )

    def start_of(way, sub):
        return pl.multiple_of(way * HALF + sub * SUB, SUB)

    def solve(way, sub):
        first = start_of(way, sub)
        rows = pl.ds(first, SUB)
        errors = solve_rows(window[rows, :].astype(F32), expand(kept_v, first) != 0, inv_v[...], cpl_v[...])
        errors_v[rows, :] = errors.astype(BF16)

    def make_factor():
        both = gath[:, pl.ds(2 * TOKENS, 16), :].astype(F32)
        factor[:, pl.ds(0, HALF)] = both[:, 0:8].reshape(WIN, HALF).astype(BF16)
        factor[:, pl.ds(HALF, HALF)] = both[:, 8:16].reshape(WIN, HALF).astype(BF16)

    def prune(way, sub):
        first = start_of(way, sub)
        rows = pl.ds(first, SUB)
        updated = w_v[rows, :].astype(F32) - jnp.dot(errors_v[rows, :], factor[...], preferred_element_type=F32)
        in_window = jnp.where(expand(scale_v, first) != 0, updated[:, :WIN], 0.0)
        w_v[rows, :] = jnp.concatenate([in_window, updated[:, WIN:]], axis=1).astype(BF16)
        pltpu.make_async_copy(w_v.at[rows], pruned.at[rows], psem.at[way * SUBS + sub]).start()

    def multiply(way, sub):
        rows = pl.ds(start_of(way, sub), SUB)
        new_left, new_right = w_v[rows, pl.ds(0, HALF)], w_v[rows, pl.ds(HALF, HALF)]

        def term(t, carry):
            sent = gath[pl.ds(t * 16, 16), pl.ds(0, 2 * TOKENS), :]
            left = sent[:, :TOKENS].reshape(16 * TOKENS, HALF)
            right = sent[:, TOKENS:].reshape(16 * TOKENS, HALF)
            dims = (((1,), (1,)), ((), ()))
            total = lax.dot_general(left, new_left, dims, preferred_element_type=F32)
            total += lax.dot_general(right, new_right, dims, preferred_element_type=F32)
            at_rows = pl.ds(pl.multiple_of(t * 16 * TOKENS, 16 * TOKENS), 16 * TOKENS)
            terms[way * SUBS + sub, at_rows, :] = total.astype(BF16)
            return carry

        lax.fori_loop(0, 2, term, 0)

    def launch(way, sub):
        ring[way, sub, 0] = terms[way * SUBS + sub, pl.ds(block_of(way, 0), BLOCK_TOKENS), :]
        piece(way, sub, 0).start()

    plan = []

    def do(when, tag, f, *a):
        if tag in ON:
            plan.append((when, len(plan), f, a))

    do(0.0, "g", first_sends)
    do(2.0, "s", squares_on)
    for j, when in ((1, 3.0), (3, 3.2), (2, 5.0)):
        do(when, "g", along_first, j)
    for j, when in ((0, 3.5), (1, 6.0), (3, 7.0), (2, 9.0)):
        do(when, "g", along_second, j, 1)
        do(when + 0.1, "g", along_second, j, 3)
        do(when + 4.0, "g", along_second, j, 2)
    do(14.0, "g", take_other)
    for n in range(HOP, HOP * (DEPTH - 1) + LINKS):
        do(TICK0 + TICK * n, "w", tick, n)
    do(6.1, "s", take_squares)
    do(6.2, "c", invert_start)
    for level in range(6):
        do(6.3 + 0.7 * level, "c", invert_level, 2**level)
    do(10.5, "c", couple)
    for sub in range(SUBS):
        do(TICK0 + TICK * (HOP * 4 + (SUB // LINK) * (sub + 1) - 1) + 0.01, "c", solve, near, sub)
    at_far = [TICK0 + TICK * (HOP * 7 + (SUB // LINK) * (sub + 1) - 1) + 0.01 for sub in range(SUBS)]
    do(14.1, "p", weight_load.wait)
    do(14.2, "p", make_factor)
    for sub in range(SUBS):
        for way, when in ((near, max(14.3, at_far[sub] - 1.0)), (1 - near, at_far[sub] + 0.1)):
            if way is not near:
                do(when, "c", solve, way, sub)
            do(when, "p", prune, way, sub)
            do(when, "t", multiply, way, sub)
            do(when, "r", launch, way, sub)
    for _, _, f, a in sorted(plan, key=lambda e: e[:2]):
        f(*a)
    if "p" not in ON:
        weight_load.wait()

    for step in range(1, DEPTH) if "r" in ON else ():
        for sub in range(SUBS):
            for way in (near, 1 - near):
                piece(way, sub, step - 1).wait_recv()
                mine = terms[way * SUBS + sub, pl.ds(block_of(way, step), BLOCK_TOKENS), :].astype(F32)
                total = (ring[way, sub, step].astype(F32) + mine).astype(BF16)
                if step < DEPTH - 1:
                    ring[way, sub, step] = total
                    piece(way, sub, step).start()
                else:
                    next_input[:, pl.ds(start_of(way, sub), SUB)] = total

    if "g" in ON:

        @pl.when(z == 0)
        def _():
            for k in range(1, DEPTH):
                square_down(k).wait_send()

    def sent_square(k, carry):
        square_across(k, r).wait_send()
        return carry

    def sent_shard(s, carry):
        shard(r, s, other).wait_send()
        return carry

    def sent_link(i, carry):
        for way in range(2):

            @pl.when(z != (DEPTH - 1 if way == 0 else 1))
            def _(way=way):
                link(way, i).wait_send()

        return carry

    def sent_piece(step, carry):
        for way in range(2):
            for sub in range(SUBS):
                piece(way, sub, step).wait_send()
        return carry

    lax.fori_loop(1, PLANE if "s" in ON else 1, sent_square, 0)
    lax.fori_loop(0, len(handed), sent_shard, 0)
    lax.fori_loop(0, LINKS if "w" in ON else 0, sent_link, 0)
    lax.fori_loop(0, DEPTH - 1 if "r" in ON else 0, sent_piece, 0)
    for i in range(2 * SUBS if "p" in ON else 0):
        rows = pl.ds(i * SUB, SUB)
        pltpu.make_async_copy(w_v.at[rows], pruned.at[rows], psem.at[i]).wait()


def per_device(weight, inverse_panel, keep_blocks, calibration):
    rows, columns = weight.shape
    anywhere = pl.BlockSpec(memory_space=pl.ANY)
    vmem = pl.BlockSpec(memory_space=pltpu.VMEM)
    dma = pltpu.SemaphoreType.DMA
    return pl.pallas_call(
        fused_kernel,
        out_shape=(
            jax.ShapeDtypeStruct((rows, columns), BF16),
            jax.ShapeDtypeStruct((BLOCK_TOKENS, rows), BF16),
        ),
        in_specs=[anywhere, anywhere, vmem, anywhere],
        out_specs=(anywhere, vmem),
        scratch_shapes=[
            pltpu.VMEM((PLANE, 2 * TOKENS + 16, HALF), BF16),
            pltpu.VMEM((rows, columns), BF16),
            pltpu.VMEM((rows, WIN), BF16),
            pltpu.VMEM((8, columns), F32),
            pltpu.VMEM((PLANE, 8, WIN), F32),
            pltpu.VMEM((WIN, WIN), F32),
            pltpu.VMEM((WIN, WIN), F32),
            pltpu.VMEM((WIN, columns), BF16),
            pltpu.VMEM((rows // TILE, WIN), jnp.int32),
            pltpu.VMEM((rows // TILE, WIN), jnp.int32),
            pltpu.VMEM((rows, WIN), BF16),
            pltpu.VMEM((2 * SUBS, PLANE * TOKENS, SUB), BF16),
            pltpu.VMEM((2, SUBS, DEPTH, BLOCK_TOKENS, SUB), BF16),
            dma((32,)), dma((PLANE,)), dma((31,)), dma((PLANE,)), dma((7,)), dma((1,)),
            dma((2, LINKS)), dma((2, LINKS)), dma((2, SUBS, DEPTH - 1)), dma((2, SUBS, DEPTH - 1)),
            dma((5,)), dma((2 * SUBS,)),
        ],
        compiler_params=pltpu.CompilerParams(
            collective_id=0, has_side_effects=True, vmem_limit_bytes=56 << 20
        ),
    )(weight, inverse_panel, keep_blocks, calibration)


def solution(mesh):
    in_specs = (P("rows", "cols"), P("rows", "cols"), P("rows", None), P("rows", "cols"))
    out_specs = (P("rows", "cols"), P("cols", "rows"))
    return jax.shard_map(
        per_device, mesh=mesh, in_specs=in_specs, out_specs=out_specs, check_vma=False
    )
```

time: 221 us -> 116 us (0.52)
  waiting for transfers between devices: 134 us -> 0 us
  Pallas kernels: 14 us -> 108 us
  blocking collectives: 24.9 us -> 0 us
  matrix products: 18.7 us -> 0 us
  between operations: 15.5 us -> 0.65 us
  local copies, waits for them, and re-layouts: 10.8 us -> 7.07 us
    pallas_call x1, Pallas kernels: 14 us -> 108 us  [per_device(): pl.pallas_call(fused_kernel, out_shape=(jax.ShapeDtypeStruct((rows, colum...]
    psum x1 -> x0, waiting for transfers between devices: 74.6 us -> none  [per_device(): lax.psum(jnp.where(owner, local_errors, jnp.zeros_like(local_errors)), 'c...]
    unnamed x4 -> x0, waiting for transfers between devices: 59.3 us -> none
    all_gather x1 -> x0, blocking collectives: 24.9 us -> none  [per_device(): lax.all_gather(inverse_panel.astype(BF16), 'rows', axis=0, tiled=True)]
    dot_general x2 -> x0, matrix products: 18.7 us -> none  [the longest x1 12.3 us: per_device(): lax.dot_general(lax.all_gather(calibration, 'rows', axis=0, tiled=True),...]
    unnamed x8 -> x5, local copies, waits for them, and re-layouts: 10 us -> 7.07 us
  transfers between devices with their start and end apart: 3 -> 0, of which waited for: 2 -> 0; matrix products, arithmetic and copies ran while one was open for 3% -> 0% of each run, Pallas kernels for 0% -> 0%
where the time goes in v1:
time: 116 us; the launch traced here: 115 us
  Pallas kernels  108 us (93%)
  local copies, waits for them, and re-layouts  7.07 us (6%)
    pallas_call x1, Pallas kernels, per_device(): pl.pallas_call(fused_kernel, out_shape=(jax.ShapeDtypeStruct((rows, colum...  108 us
    unnamed x5, local copies, waits for them, and re-layouts  7.07 us

profile of v1, /device:TPU:8, one launch (start us, length us, event | category | flops | bytes accessed | tf_op | source)
XLA Modules:
  0.0 115.4 jit_solution(10367767821079064006)
XLA Ops:
  0.6 1.4 %copy.6.keep = s32[24,4]{1,0:T(8,128)} copy(s32[24,4]{0,1:T(4,128)} %param.6) | data formatting | bytes 768 | tf_op args[2]
  2.0 107.7 %shard_map.59 = (bf16[1536,1536]{1,0:T(8,128)(2,1)}, bf16[192,1536]{1,0:T(8,128)(2,1)}) custom-call(bf16[1536,1536]{1,0:T(8,128)(2,1)} %weight.1, f32[8,1536]{1,0:T(8,128)} %panel.1, s32[24,4]{1,0:T(8,128)} %copy.6.keep, bf16[48,1536]{1,0:T(8,128)(2,1)} %calib.1), custom_call_target="tpu_custom_call" | custom-call | tf_op jit(solution)/shard_map/pallas_call | solution.py:396
  109.7 0.0 copy-start
  109.7 4.9 %copy.9 = bf16[1536,1536]{1,0:T(8,128)(2,1)} copy(bf16[1536,1536]{1,0:T(8,128)(2,1)} %get-tuple-element.4) | data formatting | bytes 9437184
  114.6 0.0 copy-done
  114.6 0.8 copy.10
Async XLA Ops:
  109.7 4.9 %copy-start = (bf16[192,1536]{1,0:T(8,128)(2,1)S(1)}, bf16[192,1536]{1,0:T(8,128)(2,1)}, u32[]{:S(2)}) copy-start(bf16[192,1536]{1,0:T(8,128)(2,1)} %get-tuple-element.5) | copy-start | bytes 1769476
